TPU v7x, 512 devices: a whole 4x4x16 slice. The times are simulated.
512 devices in a mesh: guide: 2 (over core), dp: 16 (over y, x), mp: 16 (over z).
Axes of the slice: x: 4, y: 4, z: 16, core: 2. Of those that a mesh axis runs over, the one named last changes fastest.
Arguments:
- states: bfloat16 [2, 128, 2048], P('guide', 'dp'), may hold values from -6 to 6
- lengths: int32 [2, 128], P('guide', 'dp'), may hold values from 1 to 32768, as said below
- sink_cache: bfloat16 [2, 128, 16, 2, 4, 128], P('guide', 'dp', 'mp'), may hold values from -48 to 48
- window_cache: bfloat16 [2, 128, 16, 2, 256, 128], P('guide', 'dp', 'mp'), may hold values from -360 to 360
- qkv_weight: bfloat16 [2048, 3, 16, 128], P(None, None, 'mp'), may hold values from -0.125 to 0.125
- out_weight: bfloat16 [16, 128, 2048], P('mp'), may hold values from -0.125 to 0.125
- expert_ids: int32 [2, 128, 8], replicated, may hold values from 0 to 63, all different within a row; in each aligned block of 8 rows (0 to 7, 8 to 15, ..., all dimensions but the last counted through in order) at most 2 rows name the same one
- route_weight: float32 [2, 128, 8], replicated, may hold values from 0.5 to 2
- expert_in: bfloat16 [2, 2048, 65536], P(None, None, ('guide', 'dp', 'mp')), may hold values from -0.125 to 0.125
- expert_out: bfloat16 [65536, 2048], P(('guide', 'dp', 'mp')), may hold values from -0.1875 to 0.1875
- vocab_weight: bfloat16 [2048, 26624], P(('guide', 'dp'), 'mp'), may hold values from -0.125 to 0.125
- guidance: float32 [128], P('dp'), may hold values from 1 to 5
Outputs:
- guided: float32 [128, 16, 2, 832], P('dp', 'mp', 'guide')
Inputs may be any that keep to these rules, and one draw needn't show every extreme that they name: `lengths`: one stream of one request has exactly 32768 cached positions. `expert_ids`: taking the tokens streams first, then requests, in aligned blocks of 8 tokens (the tokens of one device), no expert is named by more than 2 tokens of a block, a bound that some block reaches.
All inputs are finite; a program needn't handle non-finite values.
Results may differ from a plain program's by a relative error of at most 0.025.
Values may be sent and summed in bfloat16 or wider, within the bound.
A program may use at most 64 MiB of HBM per device.

v0:
```python
import math
import jax
import jax.numpy as jnp
from jax import lax
from jax.sharding import PartitionSpec as P

FFE = 1024
EPSILON = 1e-05


def partner(block, axis, stride):
    count = lax.axis_size(axis)
    route = []
    for low in range(count):
        high = low | 1 << stride
        if high != low and high < count:
            route += [(low, high), (high, low)]
    return lax.ppermute(block, axis, route)


def rms_norm(values):
    return values * lax.rsqrt(jnp.mean(values * values, axis=-1, keepdims=True) + EPSILON)


def rotate(vectors, positions):
    full_width = vectors.shape[-1]
    half_width = full_width // 2
    step_index = jnp.arange(half_width, dtype=jnp.float32)
    inverse = jnp.exp(step_index * (-2.0 * math.log(10000.0) / full_width))
    angles = positions.astype(jnp.float32)[:, None] * inverse[None, :]
    cosine = jnp.cos(angles)[:, None, :]
    sine_part = jnp.sin(angles)[:, None, :]
    first_half = vectors[..., :half_width]
    second = vectors[..., half_width:]
    return jnp.concatenate(
        [first_half * cosine - second * sine_part, second * cosine + first_half * sine_part],
        axis=-1,
    )


def body(
    states,
    lengths,
    sink_cache,
    window_cache,
    qkv_weight,
    out_weight,
    expert_ids,
    route_weight,
    expert_in,
    expert_out,
    vocab_weight,
    guidance,
):
    hidden = states[0]
    own_lengths = lengths[0]
    request_count = hidden.shape[0]
    normed = rms_norm(hidden.astype(jnp.float32)).astype(jnp.bfloat16)
    projected = jnp.einsum("rd,dthe->rthe", normed, qkv_weight, preferred_element_type=jnp.float32)
    query_rot = rotate(projected[:, 0], own_lengths).astype(jnp.bfloat16)
    fresh_key = rotate(projected[:, 1], own_lengths).astype(jnp.bfloat16)
    fresh_value = projected[:, 2].astype(jnp.bfloat16)
    sink_rows = sink_cache[0]
    window_rows = window_cache[0]
    sink_count = sink_rows.shape[3]
    window_count = window_rows.shape[3]
    root_size = math.sqrt(query_rot.shape[-1])
    sink_scores = (
        jnp.einsum(
            "rhe,rhse->rhs", query_rot, sink_rows[:, :, 0], preferred_element_type=jnp.float32
        )
        / root_size
    )
    window_scores = (
        jnp.einsum(
            "rhe,rhwe->rhw", query_rot, window_rows[:, :, 0], preferred_element_type=jnp.float32
        )
        / root_size
    )
    self_scores = (
        jnp.einsum("rhe,rhe->rh", query_rot, fresh_key, preferred_element_type=jnp.float32)
        / root_size
    )
    length_limit = own_lengths[:, None, None]
    sink_valid = jnp.arange(sink_count, dtype=jnp.int32)[None, None, :] < length_limit
    window_valid = (
        jnp.arange(window_count, dtype=jnp.int32)[None, None, :]
        >= sink_count + window_count - length_limit
    )
    sink_scores = jnp.where(sink_valid, sink_scores, -1e30)
    window_scores = jnp.where(window_valid, window_scores, -1e30)
    highest = jnp.maximum(
        jnp.maximum(jnp.max(sink_scores, axis=-1), jnp.max(window_scores, axis=-1)), self_scores
    )
    sink_exp = jnp.exp(sink_scores - highest[..., None])
    window_exp = jnp.exp(window_scores - highest[..., None])
    self_exp = jnp.exp(self_scores - highest)
    totals = jnp.sum(sink_exp, axis=-1) + jnp.sum(window_exp, axis=-1) + self_exp
    sink_prob = (sink_exp / totals[..., None]).astype(jnp.bfloat16)
    window_prob = (window_exp / totals[..., None]).astype(jnp.bfloat16)
    self_prob = (self_exp / totals).astype(jnp.bfloat16)
    mixture = (
        jnp.einsum(
            "rhs,rhse->rhe", sink_prob, sink_rows[:, :, 1], preferred_element_type=jnp.float32
        )
        + jnp.einsum(
            "rhw,rhwe->rhe", window_prob, window_rows[:, :, 1], preferred_element_type=jnp.float32
        )
        + self_prob[..., None].astype(jnp.float32) * fresh_value.astype(jnp.float32)
    ).astype(jnp.bfloat16)
    partial_out = jnp.einsum("rhe,hed->rd", mixture, out_weight, preferred_element_type=jnp.float32)
    attention_out = lax.psum(partial_out, "mp")
    residual = (hidden.astype(jnp.float32) + attention_out).astype(jnp.bfloat16)
    moe_in = rms_norm(residual.astype(jnp.float32)).astype(jnp.bfloat16)
    unit_count = expert_in.shape[2]
    unit_start = lax.axis_index(("guide", "dp", "mp")) * unit_count
    unit_expert = (unit_start + jnp.arange(unit_count, dtype=jnp.int32)) // FFE
    choice_rows = expert_ids.reshape(-1, expert_ids.shape[-1])
    route_rows = route_weight.reshape(-1, route_weight.shape[-1])
    coefficient = jnp.sum(
        jnp.where(
            choice_rows[:, :, None] == unit_expert[None, None, :], route_rows[:, :, None], 0.0
        ),
        axis=1,
    )
    piece = lax.all_gather(moe_in, ("guide", "dp"), axis=0, tiled=True)
    gate = jnp.dot(piece, expert_in[0], preferred_element_type=jnp.float32)
    upward = jnp.dot(piece, expert_in[1], preferred_element_type=jnp.float32)
    activated = (jax.nn.silu(gate) * upward * coefficient).astype(jnp.bfloat16)
    expert_terms = jnp.dot(activated, expert_out, preferred_element_type=jnp.float32)
    expert_part = lax.psum_scatter(expert_terms, ("guide", "dp"), scatter_dimension=0, tiled=True)
    expert_total = lax.psum(expert_part, "mp")
    final = rms_norm(residual.astype(jnp.float32) + expert_total).astype(jnp.bfloat16)
    final_all = lax.all_gather(final, ("guide", "dp"), axis=0, tiled=True)
    row_share = vocab_weight.shape[0]
    share_start = lax.axis_index(("guide", "dp")) * row_share
    final_cols = lax.dynamic_slice_in_dim(final_all, share_start, row_share, 1)
    logits = lax.psum_scatter(
        jnp.dot(final_cols, vocab_weight, preferred_element_type=jnp.float32).astype(jnp.bfloat16),
        ("guide", "dp"),
        scatter_dimension=0,
        tiled=True,
    ).astype(jnp.float32)
    half_width = logits.shape[1] // 2
    stream_index = lax.axis_index("guide")
    own_half = lax.dynamic_slice_in_dim(logits, stream_index * half_width, half_width, 1)
    other_half = lax.dynamic_slice_in_dim(logits, (1 - stream_index) * half_width, half_width, 1)
    partner_logits = partner(other_half, "guide", 0)
    is_conditional = stream_index == 0
    conditional = jnp.where(is_conditional, own_half, partner_logits)
    unconditional = jnp.where(is_conditional, partner_logits, own_half)
    guided = unconditional + guidance[:, None] * (conditional - unconditional)
    return guided.reshape(request_count, 1, 1, half_width)


def solution(mesh):
    in_specs = (
        P("guide", "dp", None),
        P("guide", "dp"),
        P("guide", "dp", "mp", None, None, None),
        P("guide", "dp", "mp", None, None, None),
        P(None, None, "mp", None),
        P("mp", None, None),
        P(),
        P(),
        P(None, None, ("guide", "dp", "mp")),
        P(("guide", "dp", "mp"), None),
        P(("guide", "dp"), "mp"),
        P("dp"),
    )
    out_specs = P("dp", "mp", "guide", None)
    return jax.shard_map(body, mesh=mesh, in_specs=in_specs, out_specs=out_specs, check_vma=False)
```

profile of v0, /device:TPU:1, one launch (start us, length us, event | category | flops | bytes accessed | tf_op | source)
XLA Modules:
  0.0 657.1 jit_solution(2036525778644055514)
XLA Ops:
  6.6 0.8 bitcast_convert_fusion
  7.4 0.8 broadcast_subtract_fusion
  8.2 0.9 fusion.23
  9.1 1.2 fusion
  12.1 0.9 fusion.11
  13.0 128.0 %all-reduce.5.cloned.1.call-done = f32[8,2048]{1,0:T(8,128)} async-done(((f32[8,2048]{1,0:T(8,128)}), f32[8,2048]{1,0:T(8,128)}) %all-reduce.5.cloned.1.call-update) | async-done | bytes 65552 | tf_op jit(solution)/shard_map/psum | solution.py:112
  141.0 1.0 fusion.26
  142.0 0.7 fusion.27
  143.1 1.3 select_reduce_fusion
  144.4 65.6 %all-gather.3.cloned.1.call-done = bf16[256,2048]{1,0:T(8,128)(2,1)} async-done(((bf16[8,2048]{1,0:T(8,128)(2,1)}), bf16[256,2048]{1,0:T(8,128)(2,1)}) %all-gather.3.cloned.1.call-update) | async-done | bytes 1048592 | tf_op jit(solution)/shard_map/all_gather | solution.py:126
  210.0 1.9 fusion.9
  211.9 3.2 fusion.4
  215.2 99.4 %reduce-scatter.2.cloned.1.call-done = f32[8,2048]{1,0:T(8,128)} async-done(((f32[256,2048]{1,0:T(8,128)}), f32[8,2048]{1,0:T(8,128)}) %reduce-scatter.2.cloned.1.call-update) | async-done | bytes 65552 | tf_op jit(solution)/shard_map/reduce_scatter | solution.py:131
  314.6 125.9 %all-reduce.7.cloned.1.call-done = f32[8,2048]{1,0:T(8,128)} async-done(((f32[8,2048]{1,0:T(8,128)}), f32[8,2048]{1,0:T(8,128)}) %all-reduce.7.cloned.1.call-update) | async-done | bytes 65552 | tf_op jit(solution)/shard_map/psum | solution.py:132
  440.5 1.0 multiply_reduce_fusion
  441.5 1.5 multiply_convert_fusion
  443.1 65.8 %all-gather.5.cloned.1.call-done = bf16[256,2048]{1,0:T(8,128)(2,1)} async-done(((bf16[8,2048]{1,0:T(8,128)(2,1)}), bf16[256,2048]{1,0:T(8,128)(2,1)}) %all-gather.5.cloned.1.call-update) | async-done | bytes 1048592 | tf_op jit(solution)/shard_map/all_gather | solution.py:134
  508.9 2.2 convolution_convert_fusion
  511.1 1.3 dynamic-slice
  513.1 132.5 %all-reduce.9.cloned.1.call-done = bf16[256,1664]{1,0:T(8,128)(2,1)} async-done(((bf16[256,1664]{1,0:T(8,128)(2,1)}), bf16[256,1664]{1,0:T(8,128)(2,1)}) %all-reduce.9.cloned.1.call-update) | async-done | bytes 851984
  645.6 0.7 dynamic-slice_convert_fusion
  646.4 2.3 collective-permute-start
  648.7 0.8 collective-permute-done
  649.6 0.6 copy.26
  (64 shorter events, 2.6 us)
Async XLA Ops:
  6.5 2.5 copy-start
  6.5 4.8 copy-start.9
  6.5 3.9 copy-start.5
  6.5 4.2 copy-start.11
  6.5 5.6 copy-start.3
  6.5 134.5 %all-reduce.5.cloned.1.call-start = ((), (), s32[]{:S(2)}) async-start(), calls=%async_computation.1 | async-start | bytes 131072 | tf_op jit(solution)/shard_map/psum | solution.py:112
  9.1 131.9 %copy-start.4 = (bf16[1,8,2048]{2,1,0:T(8,128)(2,1)S(1)}, bf16[1,8,2048]{2,1,0:T(8,128)(2,1)}, u32[]{:S(2)}) copy-start(bf16[1,8,2048]{2,1,0:T(8,128)(2,1)} %param.12) | copy-start | bytes 98308
  9.1 133.7 %copy-start.7 = (s32[2,128,8]{1,2,0:T(8,128)S(1)}, s32[2,128,8]{1,2,0:T(8,128)}, u32[]{:S(2)}) copy-start(s32[2,128,8]{1,2,0:T(8,128)} %param.18) | copy-start | bytes 24580
  10.3 132.6 %copy-start.8 = (f32[2,128,8]{1,2,0:T(8,128)S(1)}, f32[2,128,8]{1,2,0:T(8,128)}, u32[]{:S(2)}) copy-start(f32[2,128,8]{1,2,0:T(8,128)} %param.19) | copy-start | bytes 24580
  12.1 199.8 %copy-start.2 = (bf16[128,2048]{1,0:T(8,128)(2,1)S(1)}, bf16[128,2048]{1,0:T(8,128)(2,1)}, u32[]{:S(2)}) copy-start(bf16[128,2048]{1,0:T(8,128)(2,1)} %param.21) | copy-start | bytes 1572868
  13.0 197.0 %all-gather.3.cloned.1.call-start = ((), (), s32[]{:S(2)}) async-start(), calls=%async_computation.2 | async-start | bytes 1081344 | tf_op jit(solution)/shard_map/all_gather | solution.py:126
  142.7 171.9 %reduce-scatter.2.cloned.1.call-start = ((), (), s32[]{:S(2)}) async-start(), calls=%async_computation.3 | async-start | bytes 2162688 | tf_op jit(solution)/shard_map/reduce_scatter | solution.py:131
  210.0 1.9 copy-start.1
  215.1 293.8 %copy-start.6 = (bf16[64,1664]{1,0:T(8,128)(2,1)S(1)}, bf16[64,1664]{1,0:T(8,128)(2,1)}, u32[]{:S(2)}) copy-start(bf16[64,1664]{1,0:T(8,128)(2,1)} %param.22) | copy-start | bytes 638980
  215.1 434.4 %copy-start.10 = (f32[8]{0:T(128)S(1)}, f32[8]{0:T(128)}, u32[]{:S(2)}) copy-start(f32[8]{0:T(128)} %param.23) | copy-start | bytes 100
  215.1 225.4 %all-reduce.7.cloned.1.call-start = ((), (), s32[]{:S(2)}) async-start(), calls=%async_computation.4 | async-start | bytes 131072 | tf_op jit(solution)/shard_map/psum | solution.py:132
  314.6 194.3 %all-gather.5.cloned.1.call-start = ((), (), s32[]{:S(2)}) async-start(), calls=%async_computation.5 | async-start | bytes 1081344 | tf_op jit(solution)/shard_map/all_gather | solution.py:134
  443.1 202.6 %all-reduce.9.cloned.1.call-start = ((), (), s32[]{:S(2)}) async-start(), calls=%async_computation.6 | async-start | bytes 1703936
  646.4 3.1 collective-permute-start
Sparse Core Ops, SparseCore 0:
  13.1 127.8 all-reduce.4
  144.7 65.3 all-gather.2
  215.3 99.2 reduce-scatter.1
  316.9 123.6 all-reduce.6
  443.6 65.3 all-gather.4
  512.1 133.5 all-reduce.8
where the time goes:
time: 658 us; the launch traced here: 657 us
  waiting for transfers between devices  618 us (94%)
  between operations  14.4 us (2%)
  matrix products  9.92 us (2%)
  other arithmetic  9.7 us (1%)
    unnamed x7, waiting for transfers between devices  133 us
    psum x1, waiting for transfers between devices, body(): attention_out = lax.psum(partial_out, 'mp')  128 us
    psum x1, waiting for transfers between devices, body(): expert_total = lax.psum(expert_part, 'mp')  126 us
    reduce_scatter x1, waiting for transfers between devices, body(): lax.psum_scatter(expert_terms, ('guide', 'dp'), scatter_dimension=0, tile...  99.4 us
    all_gather x1, waiting for transfers between devices, body(): final_all = lax.all_gather(final, ('guide', 'dp'), axis=0, tiled=True)  65.8 us
    all_gather x1, waiting for transfers between devices, body(): piece = lax.all_gather(moe_in, ('guide', 'dp'), axis=0, tiled=True)  65.6 us
  transfers between devices with their start and end apart: 7, of which 7 were waited for; matrix products, arithmetic and copies ran while one was open for 0% of the time, Pallas kernels for 0%

commit v1 on v0

--- a/solution.py
+++ b/solution.py
@@ -129,7 +129,14 @@
     activated = (jax.nn.silu(gate) * upward * coefficient).astype(jnp.bfloat16)
     expert_terms = jnp.dot(activated, expert_out, preferred_element_type=jnp.float32)
     expert_part = lax.psum_scatter(expert_terms, ("guide", "dp"), scatter_dimension=0, tiled=True)
-    expert_total = lax.psum(expert_part, "mp")
+    total_devices = lax.axis_size("mp")
+    expert_total, answer = (expert_part, 0)
+    while 1 << answer < total_devices:
+        outer = lax.ppermute(
+            expert_total, "mp", [(dev_j, dev_j ^ 1 << answer) for dev_j in range(total_devices)]
+        )
+        expert_total = expert_total + outer
+        answer = answer + 1
     final = rms_norm(residual.astype(jnp.float32) + expert_total).astype(jnp.bfloat16)
     final_all = lax.all_gather(final, ("guide", "dp"), axis=0, tiled=True)
     row_share = vocab_weight.shape[0]

time: 658 us -> 566 us (0.86)
  waiting for transfers between devices: 618 us -> 498 us
  starting transfers between devices: 2.5 us -> 31.8 us
    psum x1 -> x0, waiting for transfers between devices: 126 us -> none  [body(): expert_total = lax.psum(expert_part, 'mp')]
    ppermute x0 -> x4, starting transfers between devices: none -> 29.4 us  [body(): lax.ppermute(expert_total, 'mp', [(dev_j, dev_j ^ 1 << answer) for dev_j...]
    ppermute x0 -> x4, waiting for transfers between devices: none -> 7.08 us  [body(): lax.ppermute(expert_total, 'mp', [(dev_j, dev_j ^ 1 << answer) for dev_j...]
    unnamed x7 -> x6, waiting for transfers between devices: 133 us -> 133 us
  transfers between devices with their start and end apart: 7 -> 10, of which waited for: 7 -> 10; matrix products, arithmetic and copies ran while one was open for 0% -> 1% of each run, Pallas kernels for 0% -> 0%
where the time goes in v1:
time: 566 us; the launch traced here: 565 us
  waiting for transfers between devices  498 us (88%)
  starting transfers between devices  31.8 us (6%)
  between operations  14.1 us (2%)
  matrix products  9.92 us (2%)
  other arithmetic  8.89 us (2%)
    unnamed x6, waiting for transfers between devices  133 us
    psum x1, waiting for transfers between devices, body(): attention_out = lax.psum(partial_out, 'mp')  128 us
    reduce_scatter x1, waiting for transfers between devices, body(): lax.psum_scatter(expert_terms, ('guide', 'dp'), scatter_dimension=0, tile...  99.4 us
    all_gather x1, waiting for transfers between devices, body(): piece = lax.all_gather(moe_in, ('guide', 'dp'), axis=0, tiled=True)  65.6 us
    all_gather x1, waiting for transfers between devices, body(): final_all = lax.all_gather(final, ('guide', 'dp'), axis=0, tiled=True)  64 us
    ppermute x4, starting transfers between devices, body(): lax.ppermute(expert_total, 'mp', [(dev_j, dev_j ^ 1 << answer) for dev_j...  29.4 us
  transfers between devices with their start and end apart: 10, of which 10 were waited for; matrix products, arithmetic and copies ran while one was open for 1% of the time, Pallas kernels for 0%

profile of v1, /device:TPU:1, one launch (start us, length us, event | category | flops | bytes accessed | tf_op | source)
XLA Modules:
  0.0 565.1 jit_solution(5490239403724983815)
XLA Ops:
  8.2 0.9 fusion.23
  9.1 1.2 fusion
  12.1 0.9 fusion.11
  13.0 128.0 %all-reduce.4.cloned.1.call-done = f32[8,2048]{1,0:T(8,128)} async-done(((f32[8,2048]{1,0:T(8,128)}), f32[8,2048]{1,0:T(8,128)}) %all-reduce.4.cloned.1.call-update) | async-done | bytes 65552 | tf_op jit(solution)/shard_map/psum | solution.py:112
  141.0 1.0 fusion.26
  143.1 1.3 select_reduce_fusion
  144.4 65.6 %all-gather.3.cloned.1.call-done = bf16[256,2048]{1,0:T(8,128)(2,1)} async-done(((bf16[8,2048]{1,0:T(8,128)(2,1)}), bf16[256,2048]{1,0:T(8,128)(2,1)}) %all-gather.3.cloned.1.call-update) | async-done | bytes 1048592 | tf_op jit(solution)/shard_map/all_gather | solution.py:126
  210.0 1.9 fusion.9
  211.9 3.2 fusion.4
  215.2 99.4 %reduce-scatter.2.cloned.1.call-done = f32[8,2048]{1,0:T(8,128)} async-done(((f32[256,2048]{1,0:T(8,128)}), f32[8,2048]{1,0:T(8,128)}) %reduce-scatter.2.cloned.1.call-update) | async-done | bytes 65552 | tf_op jit(solution)/shard_map/reduce_scatter | solution.py:131
  314.6 3.1 collective-permute-start
  317.7 2.1 collective-permute-done
  319.8 0.8 add.124
  320.6 4.2 collective-permute-start.1
  324.8 1.7 collective-permute-done.1
  326.5 7.4 %collective-permute-start.2 = (f32[8,2048]{1,0:T(8,128)S(1)}, f32[8,2048]{1,0:T(8,128)S(1)}, u32[]{:S(2)}, u32[]{:S(2)}) collective-permute-start(f32[8,2048]{1,0:T(8,128)S(1)} %add.125), channel_id=1, source_target_pairs={{0,4},{1,5},{2,6},{3,7},{4,0},{5,1},{6,2},{7,3},{8,12},{9,13},{10,... | collective-permute-start | bytes 196616 | tf_op jit(solution)/shard_map/ppermute | solution.py:135
  333.9 1.6 collective-permute-done.2
  335.6 14.7 %collective-permute-start.3 = (f32[8,2048]{1,0:T(8,128)S(1)}, f32[8,2048]{1,0:T(8,128)S(1)}, u32[]{:S(2)}, u32[]{:S(2)}) collective-permute-start(f32[8,2048]{1,0:T(8,128)S(1)} %add.126), channel_id=1, source_target_pairs={{0,8},{1,9},{2,10},{3,11},{4,12},{5,13},{6,14},{7,15},{8,0},{9,1},... | collective-permute-start | bytes 196616 | tf_op jit(solution)/shard_map/ppermute | solution.py:135
  350.3 1.6 collective-permute-done.3
  352.8 64.0 %all-gather.5.cloned.1.call-done = bf16[256,2048]{1,0:T(8,128)(2,1)} async-done(((bf16[8,2048]{1,0:T(8,128)(2,1)}), bf16[256,2048]{1,0:T(8,128)(2,1)}) %all-gather.5.cloned.1.call-update) | async-done | bytes 1048592 | tf_op jit(solution)/shard_map/all_gather | solution.py:141
  416.9 2.2 convolution_convert_fusion
  419.1 1.3 dynamic-slice
  421.0 132.9 %all-reduce.6.cloned.1.call-done = bf16[256,1664]{1,0:T(8,128)(2,1)} async-done(((bf16[256,1664]{1,0:T(8,128)(2,1)}), bf16[256,1664]{1,0:T(8,128)(2,1)}) %all-reduce.6.cloned.1.call-update) | async-done | bytes 851984
  554.7 2.3 collective-permute-start.4
  (72 shorter events, 7.9 us)
Async XLA Ops:
  6.5 2.5 copy-start
  6.5 4.8 copy-start.9
  6.5 3.9 copy-start.5
  6.5 4.2 copy-start.11
  6.5 5.6 copy-start.3
  6.5 134.5 %all-reduce.4.cloned.1.call-start = ((), (), s32[]{:S(2)}) async-start(), calls=%async_computation.1 | async-start | bytes 131072 | tf_op jit(solution)/shard_map/psum | solution.py:112
  9.1 131.9 %copy-start.4 = (bf16[1,8,2048]{2,1,0:T(8,128)(2,1)S(1)}, bf16[1,8,2048]{2,1,0:T(8,128)(2,1)}, u32[]{:S(2)}) copy-start(bf16[1,8,2048]{2,1,0:T(8,128)(2,1)} %param.12) | copy-start | bytes 98308
  9.1 133.7 %copy-start.7 = (s32[2,128,8]{1,2,0:T(8,128)S(1)}, s32[2,128,8]{1,2,0:T(8,128)}, u32[]{:S(2)}) copy-start(s32[2,128,8]{1,2,0:T(8,128)} %param.18) | copy-start | bytes 24580
  10.3 132.6 %copy-start.8 = (f32[2,128,8]{1,2,0:T(8,128)S(1)}, f32[2,128,8]{1,2,0:T(8,128)}, u32[]{:S(2)}) copy-start(f32[2,128,8]{1,2,0:T(8,128)} %param.19) | copy-start | bytes 24580
  12.1 199.8 %copy-start.2 = (bf16[128,2048]{1,0:T(8,128)(2,1)S(1)}, bf16[128,2048]{1,0:T(8,128)(2,1)}, u32[]{:S(2)}) copy-start(bf16[128,2048]{1,0:T(8,128)(2,1)} %param.21) | copy-start | bytes 1572868
  13.0 197.0 %all-gather.3.cloned.1.call-start = ((), (), s32[]{:S(2)}) async-start(), calls=%async_computation.2 | async-start | bytes 1081344 | tf_op jit(solution)/shard_map/all_gather | solution.py:126
  142.7 171.9 %reduce-scatter.2.cloned.1.call-start = ((), (), s32[]{:S(2)}) async-start(), calls=%async_computation.3 | async-start | bytes 2162688 | tf_op jit(solution)/shard_map/reduce_scatter | solution.py:131
  210.0 1.9 copy-start.1
  215.1 201.8 %copy-start.6 = (bf16[64,1664]{1,0:T(8,128)(2,1)S(1)}, bf16[64,1664]{1,0:T(8,128)(2,1)}, u32[]{:S(2)}) copy-start(bf16[64,1664]{1,0:T(8,128)(2,1)} %param.22) | copy-start | bytes 638980
  215.1 342.7 %copy-start.10 = (f32[8]{0:T(128)S(1)}, f32[8]{0:T(128)}, u32[]{:S(2)}) copy-start(f32[8]{0:T(128)} %param.23) | copy-start | bytes 100
  215.1 201.7 %all-gather.5.cloned.1.call-start = ((), (), s32[]{:S(2)}) async-start(), calls=%async_computation.4 | async-start | bytes 1081344 | tf_op jit(solution)/shard_map/all_gather | solution.py:141
  314.6 5.2 collective-permute-start
  320.6 5.9 %collective-permute-start.1 = (f32[8,2048]{1,0:T(8,128)S(1)}, f32[8,2048]{1,0:T(8,128)S(1)}, u32[]{:S(2)}, u32[]{:S(2)}) collective-permute-start(f32[8,2048]{1,0:T(8,128)S(1)} %add.124), channel_id=1, source_target_pairs={{0,2},{1,3},{2,0},{3,1},{4,6},{5,7},{6,4},{7,5},{8,10},{9,11},{10,... | collective-permute-start | bytes 196616 | tf_op jit(solution)/shard_map/ppermute | solution.py:135
  326.5 9.0 %collective-permute-start.2 = (f32[8,2048]{1,0:T(8,128)S(1)}, f32[8,2048]{1,0:T(8,128)S(1)}, u32[]{:S(2)}, u32[]{:S(2)}) collective-permute-start(f32[8,2048]{1,0:T(8,128)S(1)} %add.125), channel_id=1, source_target_pairs={{0,4},{1,5},{2,6},{3,7},{4,0},{5,1},{6,2},{7,3},{8,12},{9,13},{10,... | collective-permute-start | bytes 196616 | tf_op jit(solution)/shard_map/ppermute | solution.py:135
  335.6 16.4 %collective-permute-start.3 = (f32[8,2048]{1,0:T(8,128)S(1)}, f32[8,2048]{1,0:T(8,128)S(1)}, u32[]{:S(2)}, u32[]{:S(2)}) collective-permute-start(f32[8,2048]{1,0:T(8,128)S(1)} %add.126), channel_id=1, source_target_pairs={{0,8},{1,9},{2,10},{3,11},{4,12},{5,13},{6,14},{7,15},{8,0},{9,1},... | collective-permute-start | bytes 196616 | tf_op jit(solution)/shard_map/ppermute | solution.py:135
  352.8 201.1 %all-reduce.6.cloned.1.call-start = ((), (), s32[]{:S(2)}) async-start(), calls=%async_computation.5 | async-start | bytes 1703936
  554.7 3.1 collective-permute-start.4
Sparse Core Ops, SparseCore 0:
  13.1 127.8 all-reduce.3
  144.7 65.3 all-gather.2
  215.3 99.2 reduce-scatter.1
  352.9 63.9 all-gather.4
  420.4 133.5 all-reduce.5
